TPU v7x, 512 devices: a whole 4x4x16 slice. The times are simulated.
512 devices in a mesh: frames: 8 (over x_hi, y), queries: 64 (over x_lo, z, core).
Axes of the slice: x: 4 (x_hi: 2, x_lo: 2; x = x_hi * 2 + x_lo), y: 4, z: 16, core: 2. Of those that a mesh axis runs over, the one named last changes fastest.
Arguments:
- frame_maps: bfloat16 [16, 4096, 256], P('frames', 'queries'), may hold values from -6 to 6
- query_table: bfloat16 [8, 4096, 256], P('frames', 'queries'), may hold values from -6 to 6
- start_frame: int32 [4096], P('queries'), may hold values from 0 to 15
- row_ids: int32 [4096], P('queries'), may hold values from 0 to 63
- conv1_w: bfloat16 [3, 3, 1, 16], replicated, may hold values from -2 to 2
- conv1_b: float32 [16], replicated, may hold values from -3 to 3
- conv2_w: bfloat16 [3, 3, 16, 32], replicated, may hold values from -0.5 to 0.5
- conv2_b: float32 [32], replicated, may hold values from -3 to 3
- proj_w: bfloat16 [32, 512], replicated, may hold values from -1 to 1
- proj_b: float32 [512], replicated, may hold values from -3 to 3
- time_w: float32 [3, 512], replicated, may hold values from -3 to 3
- time_b: float32 [512], replicated, may hold values from -3 to 3
Outputs:
- track_feats: bfloat16 [4096, 16, 512], P('queries', 'frames')
Inputs may be any that keep to these rules, and one draw needn't show every extreme that they name: `start_frame`: the frame in which the query was picked, one of the 16 frames. `row_ids`: a row index within the query's own block of 64 rows.
All inputs are finite; a program needn't handle non-finite values.
Results may differ from a plain program's by a relative error of at most 0.001.
The roundings to bfloat16 on the way count: a program that leaves them out, or rounds other values in their place, can miss the bound.
Values may be sent and summed in bfloat16 or wider, within the bound.
No kernel may reach another device: no remote copies, remote signals or barrier semaphores. Data moves between devices by JAX's collectives and lax.ppermute only.
A program may use at most 64 MiB of HBM per device.

v0:
```python
import jax
import jax.numpy as jnp
from jax import lax
from jax.sharding import PartitionSpec as P

MAP = 64
CH2 = 32


def padded(block, sides, width):
    for axis, dim in sides:
        count = lax.axis_size(axis)
        forward = [(i, i + 1) for i in range(count - 1)]
        backward = [(target, source) for source, target in forward]
        low = lax.ppermute(
            lax.slice_in_dim(block, block.shape[dim] - width, None, axis=dim), axis, forward
        )
        high = lax.ppermute(lax.slice_in_dim(block, 0, width, axis=dim), axis, backward)
        block = jnp.concatenate([low, block, high], axis=dim)
    return block


def per_device(
    frame_maps,
    query_table,
    start_frame,
    row_ids,
    conv1_w,
    conv1_b,
    conv2_w,
    conv2_b,
    proj_w,
    proj_b,
    time_w,
    time_b,
):
    frames_here = frame_maps.shape[0]
    frame_block = lax.axis_index("frames")
    own_rows = query_table[0][row_ids]
    owned = start_frame // frames_here == frame_block
    own_term = jnp.where(owned[:, None], own_rows.astype(jnp.float32), 0.0)
    queries = lax.psum(own_term.astype(jnp.bfloat16), "frames")
    query_count = queries.shape[0]
    every_query = lax.all_gather(queries, "queries", axis=0, tiled=True)
    band = (
        jnp.einsum("frc,qc->rfq", frame_maps, every_query, preferred_element_type=jnp.float32)
        * 0.0625
    ).astype(jnp.bfloat16)
    costs = lax.all_to_all(band, "queries", split_axis=2, concat_axis=0, tiled=True)
    block_size = min(64, query_count)
    block_count = query_count // block_size
    pooled_init = jnp.zeros((CH2, frames_here, query_count), jnp.bfloat16)

    def one_block(block_index, pooled_acc):
        images = costs.reshape(MAP, MAP, 1, frames_here * block_size)
        layer_one = lax.conv_general_dilated(
            images,
            conv1_w,
            (2, 2),
            ((1, 1), (1, 1)),
            dimension_numbers=("HWCN", "HWIO", "HWCN"),
            preferred_element_type=jnp.float32,
        )
        layer_one = jax.nn.relu(layer_one + conv1_b[None, None, :, None]).astype(jnp.bfloat16)
        layer_two = lax.conv_general_dilated(
            layer_one,
            conv2_w,
            (2, 2),
            ((1, 1), (1, 1)),
            dimension_numbers=("HWCN", "HWIO", "HWCN"),
            preferred_element_type=jnp.float32,
        )
        layer_two = jax.nn.relu(layer_two + conv2_b[None, None, :, None])
        pooled_block = (
            jnp.mean(layer_two, axis=(0, 1))
            .astype(jnp.bfloat16)
            .reshape(CH2, frames_here, block_size)
        )
        return pooled_block

    pooled = lax.fori_loop(0, block_count, one_block, pooled_init)
    projected = padded(
        (
            jnp.einsum("cfq,cd->qfd", pooled, proj_w, preferred_element_type=jnp.float32) + proj_b
        ).astype(jnp.bfloat16),
        (("frames", 1),),
        1,
    )
    widened_f32 = projected.astype(jnp.float32)
    mixed = (
        time_w[0] * widened_f32[:, :-2]
        + time_w[1] * widened_f32[:, 1:-1]
        + time_w[2] * widened_f32[:, 2:]
        + time_b
    )
    return mixed.astype(jnp.bfloat16)


def solution(mesh):
    placed = (
        P("frames", "queries", None),
        P("frames", "queries", None),
        P("queries"),
        P("queries"),
        P(),
        P(),
        P(),
        P(),
        P(),
        P(),
        P(),
        P(),
    )
    return jax.shard_map(
        per_device,
        mesh=mesh,
        in_specs=placed,
        out_specs=P("queries", "frames", None),
        check_vma=False,
    )
```

profile of v0, /device:TPU:57, one launch (start us, length us, event | category | flops | bytes accessed | tf_op | source)
XLA Modules:
  0.0 289.6 jit_solution(6858478085503585251)
XLA Ops:
  6.5 0.0 copy-start
  6.5 0.0 all-gather.2.cloned.1.call-start
  6.5 0.7 compare_select_fusion
  7.2 1.4 gather_fusion
  8.7 0.7 fusion.18
  9.3 0.1 select_convert_fusion
  9.4 29.9 %psum.7 = bf16[64,256]{1,0:T(8,128)(2,1)} all-reduce(bf16[64,256]{1,0:T(8,128)(2,1)S(1)} %select_convert_fusion), channel_id=1, replica_groups=mesh['frames'=8,'queries'=64] {'frames'}, use_global_device_ids=true, to_apply=%region_0.1 | all-reduce | flops 16384 | bytes 65536 | tf_op jit(solution)/shard_map/psum | solution.py:42
  39.3 0.0 all-gather.2.cloned.1.call-update
  39.4 134.6 %all-gather.2.cloned.1.call-done = bf16[4096,256]{1,0:T(8,128)(2,1)} async-done(((bf16[64,256]{1,0:T(8,128)(2,1)}), bf16[4096,256]{1,0:T(8,128)(2,1)}) %all-gather.2.cloned.1.call-update) | async-done | bytes 2097168 | tf_op jit(solution)/shard_map/all_gather | solution.py:44
  174.0 0.0 copy-done
  174.0 2.4 fusion.1
  176.4 2.8 copy.21
  179.2 1.5 reshape.32
  180.7 63.0 %all_to_all.15 = bf16[64,2,4096]{2,1,0:T(2,128)(2,1)} all-to-all(bf16[64,2,4096]{2,1,0:T(2,128)(2,1)S(1)} %reshape.32), channel_id=1, replica_groups=mesh['frames'=8,'queries'=64] {'queries'}, dimensions={0} | all-to-all | bytes 2097152 | tf_op jit(solution)/shard_map/all_to_all | solution.py:49
  243.8 5.1 %reshape.33 = bf16[4096,2,64]{2,1,0:T(2,128)(2,1)S(1)} reshape(bf16[64,2,4096]{2,1,0:T(2,128)(2,1)} %all_to_all.15) | data formatting | bytes 2097152
  248.8 6.4 %copy.22 = bf16[64,2,64,64]{3,1,0,2:T(2,128)(2,1)} copy(bf16[64,2,64,64]{0,1,3,2:T(2,128)(2,1)S(1)} %bitcast.22) | data formatting | bytes 2097152 | tf_op jit(solution)/shard_map/all_to_all | solution.py:49
  255.3 7.8 %reshape.31 = bf16[64,64,1,128]{3,2,1,0:T(2,128)(2,1)S(1)} reshape(bf16[64,64,2,64]{3,2,1,0:T(2,128)(2,1)} %bitcast.23) | data formatting | bytes 2097152 | tf_op jit(solution)/shard_map/while/body/eval_jaxpr/reshape | solution.py:55
  263.1 0.0 copy-done.5
  263.1 0.0 copy-start.1
  263.1 0.0 copy-start.3
  263.1 0.0 copy-start.2
  263.2 0.0 copy-start.4
  263.2 5.5 %maximum_reduce_fusion = f32[32,128]{1,0:T(8,128)S(1)} fusion(f32[32]{0:T(128)S(1)} %copy-done.7, bf16[3,3,16,32]{3,2,1,0:T(8,128)(2,1)S(1)} %copy-done.5, f32[16]{0:T(128)S(1)} %copy-done.8, bf16[64,64,1,128]{3,2,1,0:T(2,128)(2,1)S(1)} %reshape.31, bf16[3,3,1,16]{3,1,2,0:T(4,128)(2,1)S(1)} %copy-done.6), kind=kOutput, calls=%fused_computation.6 | convolution fusion | flops 335937536 | bytes 1074656 | tf_op jit(solution)/shard_map/while/body/eval_jaxpr/conv_general_dilated | solution.py:65
  268.7 0.1 convert_element_type.42
  268.7 0.2 fusion.9
  269.0 4.2 %collective-permute-start = (bf16[64,1,512]{2,0,1:T(8,128)(2,1)S(1)}, bf16[64,1,512]{2,0,1:T(8,128)(2,1)S(1)}, u32[]{:S(2)}, u32[]{:S(2)}) collective-permute-start(bf16[64,1,512]{2,0,1:T(8,128)(2,1)S(1)} %get-tuple-element.16), channel_id=1, source_target_pairs={{0,64},{64,128},{128,192},{192,256},{256,320},{320,384},{384,448},... | collective-permute-start | bytes 196616 | tf_op jit(solution)/shard_map/ppermute | solution.py:15
  273.2 1.9 collective-permute-start.1
  275.2 0.0 copy-done.2
  275.2 0.0 collective-permute-done
  275.2 6.7 %collective-permute-done.1 = bf16[64,1,512]{2,0,1:T(8,128)(2,1)S(1)} collective-permute-done((bf16[64,1,512]{2,0,1:T(8,128)(2,1)S(1)}, bf16[64,1,512]{2,0,1:T(8,128)(2,1)S(1)}, u32[]{:S(2)}, u32[]{:S(2)}) %collective-permute-start.1) | collective-permute-done | bytes 65568 | tf_op jit(solution)/shard_map/ppermute | solution.py:18
  281.9 0.1 fusion.12
  282.0 0.8 copy.26
  (15 shorter events, 0.1 us)
Async XLA Ops:
  6.5 167.4 %copy-start = (bf16[2,64,256]{2,1,0:T(8,128)(2,1)S(1)}, bf16[2,64,256]{2,1,0:T(8,128)(2,1)}, u32[]{:S(2)}) copy-start(bf16[2,64,256]{2,1,0:T(8,128)(2,1)} %param.12) | copy-start | bytes 196612
  6.5 167.4 %all-gather.2.cloned.1.call-start = ((), (), s32[]{:S(2)}) async-start(), calls=%async_computation.1 | async-start | bytes 2129920 | tf_op jit(solution)/shard_map/all_gather | solution.py:44
  255.3 7.8 %copy-start.5 = (bf16[3,3,16,32]{3,2,1,0:T(8,128)(2,1)S(1)}, bf16[3,3,16,32]{3,2,1,0:T(8,128)(2,1)}, u32[]{:S(2)}) copy-start(bf16[3,3,16,32]{3,2,1,0:T(8,128)(2,1)} %param.18) | copy-start | bytes 27652
  255.3 7.8 %copy-start.6 = (bf16[3,3,1,16]{3,1,2,0:T(4,128)(2,1)S(1)}, bf16[3,3,1,16]{3,1,2,0:T(4,128)(2,1)}, u32[]{:S(2)}) copy-start(bf16[3,3,1,16]{3,1,2,0:T(4,128)(2,1)} %param.16) | copy-start | bytes 868
  255.3 7.8 %copy-start.7 = (f32[32]{0:T(128)S(1)}, f32[32]{0:T(128)}, u32[]{:S(2)}) copy-start(f32[32]{0:T(128)} %param.19) | copy-start | bytes 388
  255.3 7.8 %copy-start.8 = (f32[16]{0:T(128)S(1)}, f32[16]{0:T(128)}, u32[]{:S(2)}) copy-start(f32[16]{0:T(128)} %param.17) | copy-start | bytes 196
  263.1 5.6 %copy-start.1 = (bf16[32,512]{1,0:T(8,128)(2,1)S(1)}, bf16[32,512]{1,0:T(8,128)(2,1)}, u32[]{:S(2)}) copy-start(bf16[32,512]{1,0:T(8,128)(2,1)} %param.20) | copy-start | bytes 98308
  263.1 5.6 %copy-start.3 = (f32[512]{0:T(512)S(1)}, f32[512]{0:T(512)}, u32[]{:S(2)}) copy-start(f32[512]{0:T(512)} %param.21) | copy-start | bytes 6148
  263.1 12.0 %copy-start.2 = (f32[3,512]{1,0:T(4,128)S(1)}, f32[3,512]{1,0:T(4,128)}, u32[]{:S(2)}) copy-start(f32[3,512]{1,0:T(4,128)} %param.22) | copy-start | bytes 18436
  263.2 18.8 %copy-start.4 = (f32[512]{0:T(512)S(1)}, f32[512]{0:T(512)}, u32[]{:S(2)}) copy-start(f32[512]{0:T(512)} %param.23) | copy-start | bytes 6148
  269.0 6.2 %collective-permute-start = (bf16[64,1,512]{2,0,1:T(8,128)(2,1)S(1)}, bf16[64,1,512]{2,0,1:T(8,128)(2,1)S(1)}, u32[]{:S(2)}, u32[]{:S(2)}) collective-permute-start(bf16[64,1,512]{2,0,1:T(8,128)(2,1)S(1)} %get-tuple-element.16), channel_id=1, source_target_pairs={{0,64},{64,128},{128,192},{192,256},{256,320},{320,384},{384,448},... | collective-permute-start | bytes 196616 | tf_op jit(solution)/shard_map/ppermute | solution.py:15
  273.2 8.6 %collective-permute-start.1 = (bf16[64,1,512]{2,0,1:T(8,128)(2,1)S(1)}, bf16[64,1,512]{2,0,1:T(8,128)(2,1)S(1)}, u32[]{:S(2)}, u32[]{:S(2)}) collective-permute-start(bf16[64,1,512]{2,0,1:T(8,128)(2,1)S(1)} %get-tuple-element.17), channel_id=1, source_target_pairs={{64,0},{128,64},{192,128},{256,192},{320,256},{384,320},{448,384},... | collective-permute-start | bytes 196616 | tf_op jit(solution)/shard_map/ppermute | solution.py:18
Sparse Core Ops, SparseCore 0:
  39.5 134.4 all-gather.1
where the time goes:
time: 290 us
  waiting for transfers between devices  141 us (49%)
  blocking collectives  93 us (32%)
  local copies, waits for them, and re-layouts  26 us (9%)
  between operations  13.6 us (5%)
  matrix products  8.08 us (3%)
  starting transfers between devices  6.17 us (2%)
    all_gather x1, waiting for transfers between devices, per_device(): every_query = lax.all_gather(queries, 'queries', axis=0, tiled=True)  135 us
    all_to_all x1, blocking collectives, per_device(): lax.all_to_all(band, 'queries', split_axis=2, concat_axis=0, tiled=True)  63 us
    psum x1, blocking collectives, per_device(): queries = lax.psum(own_term.astype(jnp.bfloat16), 'frames')  29.9 us
    reshape x1, local copies, waits for them, and re-layouts, one_block(): images = costs.reshape(MAP, MAP, 1, frames_here * block_size)  7.79 us
    ppermute x1, waiting for transfers between devices, padded(): lax.ppermute(lax.slice_in_dim(block, 0, width, axis=dim), axis, backward)  6.66 us
    unnamed x20, local copies, waits for them, and re-layouts  6.6 us
    all_to_all x1, local copies, waits for them, and re-layouts, per_device(): lax.all_to_all(band, 'queries', split_axis=2, concat_axis=0, tiled=True)  6.44 us
  transfers between devices with their start and end apart: 3, of which 2 were waited for; matrix products, arithmetic and copies ran while one was open for 0% of the time, Pallas kernels for 0%

commit v1 on v0

--- a/solution.py
+++ b/solution.py
@@ -41,7 +41,9 @@
     own_term = jnp.where(owned[:, None], own_rows.astype(jnp.float32), 0.0)
     queries = lax.psum(own_term.astype(jnp.bfloat16), "frames")
     query_count = queries.shape[0]
-    every_query = lax.all_gather(queries, "queries", axis=0, tiled=True)
+    every_query = jnp.concatenate(
+        lax.all_to_all(jnp.stack([queries] * lax.axis_size("queries")), "queries", 0, 0), axis=0
+    )
     band = (
         jnp.einsum("frc,qc->rfq", frame_maps, every_query, preferred_element_type=jnp.float32)
         * 0.0625

time: 290 us -> 264 us (0.910)
  waiting for transfers between devices: 141 us -> 6.66 us
  blocking collectives: 93 us -> 212 us
  between operations: 13.6 us -> 0.2 us
  starting transfers between devices: 6.17 us -> 10 us
    all_gather x1 -> x0, waiting for transfers between devices: 135 us -> none  [per_device(): every_query = lax.all_gather(queries, 'queries', axis=0, tiled=True)]
    all_to_all x0 -> x1, blocking collectives: none -> 122 us  [per_device(): lax.all_to_all(jnp.stack([queries] * lax.axis_size('queries')), 'queries'...]
    ppermute x1, starting transfers between devices: 4.24 us -> 8.13 us  [padded(): lax.ppermute(lax.slice_in_dim(block, block.shape[dim] - width, None, axis...]
  transfers between devices with their start and end apart: 3 -> 2, of which waited for: 2 -> 1; matrix products, arithmetic and copies ran while one was open for 0% -> 0% of each run, Pallas kernels for 0% -> 0%
where the time goes in v1:
time: 264 us; the launch traced here: 263 us
  blocking collectives  212 us (80%)
  local copies, waits for them, and re-layouts  26.2 us (10%)
  starting transfers between devices  10 us (4%)
  waiting for transfers between devices  6.66 us (3%)
  matrix products  6.5 us (2%)
    all_to_all x1, blocking collectives, per_device(): lax.all_to_all(jnp.stack([queries] * lax.axis_size('queries')), 'queries'...  122 us
    all_to_all x1, blocking collectives, per_device(): lax.all_to_all(band, 'queries', split_axis=2, concat_axis=0, tiled=True)  61.2 us
    psum x1, blocking collectives, per_device(): queries = lax.psum(own_term.astype(jnp.bfloat16), 'frames')  29.3 us
    ppermute x1, starting transfers between devices, padded(): lax.ppermute(lax.slice_in_dim(block, block.shape[dim] - width, None, axis...  8.13 us
    reshape x1, local copies, waits for them, and re-layouts, one_block(): images = costs.reshape(MAP, MAP, 1, frames_here * block_size)  7.79 us
    ppermute x1, waiting for transfers between devices, padded(): lax.ppermute(lax.slice_in_dim(block, 0, width, axis=dim), axis, backward)  6.66 us
    unnamed x20, local copies, waits for them, and re-layouts  6.6 us
    all_to_all x1, local copies, waits for them, and re-layouts, per_device(): lax.all_to_all(band, 'queries', split_axis=2, concat_axis=0, tiled=True)  6.43 us
  transfers between devices with their start and end apart: 2, of which 1 were waited for; matrix products, arithmetic and copies ran while one was open for 0% of the time, Pallas kernels for 0%

profile of v1, /device:TPU:57, one launch (start us, length us, event | category | flops | bytes accessed | tf_op | source)
XLA Modules:
  0.0 263.3 jit_solution(15751702252090498787)
XLA Ops:
  0.0 0.0 copy-start
  0.0 0.7 compare_select_fusion
  0.7 1.4 gather_fusion
  2.1 0.7 fusion.17
  2.8 0.1 select_convert_fusion
  2.9 29.3 %psum.7 = bf16[64,256]{1,0:T(8,128)(2,1)S(1)} all-reduce(bf16[64,256]{1,0:T(8,128)(2,1)S(1)} %select_convert_fusion), channel_id=1, replica_groups=mesh['frames'=8,'queries'=64] {'frames'}, use_global_device_ids=true, to_apply=%region_0.1 | all-reduce | flops 16384 | bytes 65536 | tf_op jit(solution)/shard_map/psum | solution.py:42
  32.2 0.2 stack.2
  32.4 121.6 %all_to_all.20 = bf16[64,64,256]{2,1,0:T(8,128)(2,1)S(1)} all-to-all(bf16[64,64,256]{2,1,0:T(8,128)(2,1)S(1)} %stack.2), channel_id=1, replica_groups=mesh['frames'=8,'queries'=64] {'queries'}, dimensions={0} | all-to-all | bytes 4194304 | tf_op jit(solution)/shard_map/all_to_all | solution.py:45
  154.0 0.0 copy-done
  154.0 0.8 fusion.1
  154.8 2.8 %copy.21 = bf16[64,2,4096]{0,1,2:T(2,128)(2,1)S(1)} copy(bf16[64,2,4096]{2,0,1:T(8,128)(2,1)S(1)} %fusion.1) | data formatting | bytes 2097152 | tf_op jit(solution)/shard_map/convert_element_type | solution.py:50
  157.7 1.5 reshape.38
  159.2 61.2 %all_to_all.21 = bf16[64,2,4096]{2,1,0:T(2,128)(2,1)} all-to-all(bf16[64,2,4096]{2,1,0:T(2,128)(2,1)S(1)} %reshape.38), channel_id=1, replica_groups=mesh['frames'=8,'queries'=64] {'queries'}, dimensions={0} | all-to-all | bytes 2097152 | tf_op jit(solution)/shard_map/all_to_all | solution.py:51
  220.4 5.1 %reshape.39 = bf16[4096,2,64]{2,1,0:T(2,128)(2,1)S(1)} reshape(bf16[64,2,4096]{2,1,0:T(2,128)(2,1)} %all_to_all.21) | data formatting | bytes 2097152
  225.5 6.4 %copy.22 = bf16[64,2,64,64]{3,1,0,2:T(2,128)(2,1)} copy(bf16[64,2,64,64]{0,1,3,2:T(2,128)(2,1)S(1)} %bitcast.23) | data formatting | bytes 2097152 | tf_op jit(solution)/shard_map/all_to_all | solution.py:51
  231.9 7.8 %reshape.37 = bf16[64,64,1,128]{3,2,1,0:T(2,128)(2,1)S(1)} reshape(bf16[64,64,2,64]{3,2,1,0:T(2,128)(2,1)} %bitcast.24) | data formatting | bytes 2097152 | tf_op jit(solution)/shard_map/while/body/eval_jaxpr/reshape | solution.py:57
  239.7 0.0 copy-done.5
  239.7 0.0 copy-done.6
  239.7 0.0 copy-done.7
  239.7 0.0 copy-start.1
  239.7 0.0 copy-start.3
  239.7 0.0 copy-start.2
  239.7 0.0 copy-start.4
  239.8 5.5 %maximum_reduce_fusion = f32[32,128]{1,0:T(8,128)S(1)} fusion(f32[32]{0:T(128)S(1)} %copy-done.7, bf16[3,3,16,32]{3,2,1,0:T(8,128)(2,1)S(1)} %copy-done.5, f32[16]{0:T(128)S(1)} %copy-done.8, bf16[64,64,1,128]{3,2,1,0:T(2,128)(2,1)S(1)} %reshape.37, bf16[3,3,1,16]{3,1,2,0:T(4,128)(2,1)S(1)} %copy-done.6), kind=kOutput, calls=%fused_computation.6 | convolution fusion | flops 335937536 | bytes 1074656 | tf_op jit(solution)/shard_map/while/body/eval_jaxpr/conv_general_dilated | solution.py:67
  245.2 0.1 convert_element_type.42
  245.3 0.2 fusion.8
  245.6 8.1 %collective-permute-start = (bf16[64,1,512]{2,0,1:T(8,128)(2,1)S(1)}, bf16[64,1,512]{2,0,1:T(8,128)(2,1)S(1)}, u32[]{:S(2)}, u32[]{:S(2)}) collective-permute-start(bf16[64,1,512]{2,0,1:T(8,128)(2,1)S(1)} %get-tuple-element.16), channel_id=1, source_target_pairs={{0,64},{64,128},{128,192},{192,256},{256,320},{320,384},{384,448},... | collective-permute-start | bytes 196616 | tf_op jit(solution)/shard_map/ppermute | solution.py:15
  253.7 1.9 collective-permute-start.1
  255.7 0.0 collective-permute-done
  255.7 6.7 %collective-permute-done.1 = bf16[64,1,512]{2,0,1:T(8,128)(2,1)S(1)} collective-permute-done((bf16[64,1,512]{2,0,1:T(8,128)(2,1)S(1)}, bf16[64,1,512]{2,0,1:T(8,128)(2,1)S(1)}, u32[]{:S(2)}, u32[]{:S(2)}) %collective-permute-start.1) | collective-permute-done | bytes 65568 | tf_op jit(solution)/shard_map/ppermute | solution.py:18
  262.4 0.1 fusion.11
  262.5 0.8 copy.26
  (14 shorter events, 0.1 us)
Async XLA Ops:
  0.0 154.0 %copy-start = (bf16[2,64,256]{2,1,0:T(8,128)(2,1)S(1)}, bf16[2,64,256]{2,1,0:T(8,128)(2,1)}, u32[]{:S(2)}) copy-start(bf16[2,64,256]{2,1,0:T(8,128)(2,1)} %param.12) | copy-start | bytes 196612
  231.9 7.8 %copy-start.5 = (bf16[3,3,16,32]{3,2,1,0:T(8,128)(2,1)S(1)}, bf16[3,3,16,32]{3,2,1,0:T(8,128)(2,1)}, u32[]{:S(2)}) copy-start(bf16[3,3,16,32]{3,2,1,0:T(8,128)(2,1)} %param.18) | copy-start | bytes 27652
  231.9 7.8 %copy-start.6 = (bf16[3,3,1,16]{3,1,2,0:T(4,128)(2,1)S(1)}, bf16[3,3,1,16]{3,1,2,0:T(4,128)(2,1)}, u32[]{:S(2)}) copy-start(bf16[3,3,1,16]{3,1,2,0:T(4,128)(2,1)} %param.16) | copy-start | bytes 868
  231.9 7.8 %copy-start.7 = (f32[32]{0:T(128)S(1)}, f32[32]{0:T(128)}, u32[]{:S(2)}) copy-start(f32[32]{0:T(128)} %param.19) | copy-start | bytes 388
  231.9 7.8 %copy-start.8 = (f32[16]{0:T(128)S(1)}, f32[16]{0:T(128)}, u32[]{:S(2)}) copy-start(f32[16]{0:T(128)} %param.17) | copy-start | bytes 196
  239.7 5.6 %copy-start.1 = (bf16[32,512]{1,0:T(8,128)(2,1)S(1)}, bf16[32,512]{1,0:T(8,128)(2,1)}, u32[]{:S(2)}) copy-start(bf16[32,512]{1,0:T(8,128)(2,1)} %param.20) | copy-start | bytes 98308
  239.7 5.6 %copy-start.3 = (f32[512]{0:T(512)S(1)}, f32[512]{0:T(512)}, u32[]{:S(2)}) copy-start(f32[512]{0:T(512)} %param.21) | copy-start | bytes 6148
  239.7 15.9 %copy-start.2 = (f32[3,512]{1,0:T(4,128)S(1)}, f32[3,512]{1,0:T(4,128)}, u32[]{:S(2)}) copy-start(f32[3,512]{1,0:T(4,128)} %param.22) | copy-start | bytes 18436
  239.7 22.6 %copy-start.4 = (f32[512]{0:T(512)S(1)}, f32[512]{0:T(512)}, u32[]{:S(2)}) copy-start(f32[512]{0:T(512)} %param.23) | copy-start | bytes 6148
  245.6 10.1 %collective-permute-start = (bf16[64,1,512]{2,0,1:T(8,128)(2,1)S(1)}, bf16[64,1,512]{2,0,1:T(8,128)(2,1)S(1)}, u32[]{:S(2)}, u32[]{:S(2)}) collective-permute-start(bf16[64,1,512]{2,0,1:T(8,128)(2,1)S(1)} %get-tuple-element.16), channel_id=1, source_target_pairs={{0,64},{64,128},{128,192},{192,256},{256,320},{320,384},{384,448},... | collective-permute-start | bytes 196616 | tf_op jit(solution)/shard_map/ppermute | solution.py:15
  253.7 8.6 %collective-permute-start.1 = (bf16[64,1,512]{2,0,1:T(8,128)(2,1)S(1)}, bf16[64,1,512]{2,0,1:T(8,128)(2,1)S(1)}, u32[]{:S(2)}, u32[]{:S(2)}) collective-permute-start(bf16[64,1,512]{2,0,1:T(8,128)(2,1)S(1)} %get-tuple-element.17), channel_id=1, source_target_pairs={{64,0},{128,64},{192,128},{256,192},{320,256},{384,320},{448,384},... | collective-permute-start | bytes 196616 | tf_op jit(solution)/shard_map/ppermute | solution.py:18
